TPU v7x, 256 devices: a whole 4x4x8 slice. The times are simulated.
256 devices in a mesh: sec: 2 (over y_lo), grp: 16 (over z, y_hi), tp: 8 (over x, core).
Axes of the slice: x: 4, y: 4 (y_hi: 2, y_lo: 2; y = y_hi * 2 + y_lo), z: 8, core: 2. Of those that a mesh axis runs over, the one named last changes fastest.
Arguments:
- hidden_in: bfloat16 [1024, 7168], P(('sec', 'grp', 'tp')), may hold values from -6 to 6
- queries: bfloat16 [1024, 16, 8, 576], P(('sec', 'grp'), None, 'tp'), may hold values from -61 to 61
- latent_cache: bfloat16 [1024, 64, 576], P(('sec', 'grp')), may hold values from -6 to 6
- lengths: int32 [1024], P(('sec', 'grp')), may hold values from 2 to 64, as said below
- w_uv: bfloat16 [16, 8, 512, 128], P(None, 'tp'), may hold values from -0.75 to 0.75
- attn_weight: bfloat16 [16, 8, 128, 7168], P(None, 'tp', None, 'grp'), may hold values from -0.125 to 0.125
- norm_gain: float32 [7168], replicated, may hold values from 0.1 to 1.9
- router: bfloat16 [7168, 32], replicated, may hold values from -0.0625 to 0.0625
- routes: int32 [1024, 8], P(('sec', 'grp', 'tp')), may hold values from 0 to 31, all different within a row; in each aligned block of 4 rows (0 to 3, 4 to 7, ...) at most 2 rows name the same one
- live_counts: int32 [256], P(('sec', 'grp', 'tp')), may hold values from 3 to 4, as said below
- expert_in: bfloat16 [32, 7168, 2, 1024], P(('sec', 'grp'), None, None, 'tp'), may hold values from -0.0625 to 0.0625
- expert_out: bfloat16 [32, 1024, 7168], P(('sec', 'grp'), 'tp'), may hold values from -0.5 to 0.5
Outputs:
- layer_out: bfloat16 [1024, 7168], P(('sec', 'grp', 'tp'))
Inputs may be any that keep to these rules, and one draw needn't show every extreme that they name: `lengths`: some request has exactly 64 cached positions and some has 2. `live_counts`: some device has all 4 slots live and some has exactly 3. `routes`: the 8 experts of a token differ. Within the rows of one device (aligned blocks of 4 rows) no expert is named by more than 2 rows, a bound that some block reaches.
All inputs are finite; a program needn't handle non-finite values.
Results may differ from a plain program's by a relative error of at most 0.018.
Values may be sent and summed in bfloat16 or wider, within the bound.
No kernel may reach another device: no remote copies, remote signals or barrier semaphores. Data moves between devices by JAX's collectives and lax.ppermute only.
A program may use at most 64 MiB of HBM per device.

v0:
```python
import jax
import jax.numpy as jnp
from jax import lax
from jax.sharding import Mesh
from jax.sharding import PartitionSpec as P

GRP = ("grp_0", "grp_1")
SEC_GRP = ("sec", "grp_0", "grp_1")
GRP_SEC = ("grp_0", "grp_1", "sec")
SEC_GRP_TP = ("sec", "grp_0", "grp_1", "tp")
score_scale = 192.0 ** (-0.5)
route_scale = 2.5


def gathered_by_axis(x, axes, dim):
    out = x
    for number in range(len(axes) - 1, -1, -1):
        out = lax.all_gather(out, axes[number], axis=dim, tiled=True)
    return out


def in_blocks(x, dim, peers):
    lengths = x.shape
    tiles = x.reshape(*lengths[:dim], peers, lengths[dim] // peers, *lengths[dim + 1 :])
    return jnp.moveaxis(tiles, dim, 0)


def sent_and_summed(x, axis, dim):
    tiles = in_blocks(x, dim, lax.axis_size(axis))
    arrived = lax.all_to_all(tiles, axis, split_axis=0, concat_axis=0, tiled=True)
    return arrived.astype(jnp.float32).sum(axis=0)


def in_order(tiles, dim):
    tiles = jnp.moveaxis(tiles, 0, dim)
    lengths = tiles.shape
    return tiles.reshape(*lengths[:dim], lengths[dim] * lengths[dim + 1], *lengths[dim + 2 :])


def exchange_both(x, axis, axes, splits, concats):
    sizes = [lax.axis_size(a) for a in axes]
    tiles = in_blocks(x, splits[0], sizes[0])
    tiles = jnp.moveaxis(in_blocks(tiles, splits[1] + 1, sizes[1]), 0, 1)
    inside = tiles.shape[2:]
    tiles = tiles.reshape(-1, *inside)
    tiles = lax.all_to_all(tiles, axis, split_axis=0, concat_axis=0, tiled=True)
    tiles = in_order(tiles.reshape(*sizes, *inside), concats[0] + 1)
    return in_order(tiles, concats[1])


def expert_slice(rows_in, expert_in, expert_out):
    width = rows_in.shape[1]
    slice_width = expert_in.shape[3]
    gate_up = jnp.dot(
        rows_in, expert_in[0].reshape(width, 2 * slice_width), preferred_element_type=jnp.float32
    )
    activated = (jax.nn.silu(gate_up[:, :slice_width]) * gate_up[:, slice_width:]).astype(
        jnp.bfloat16
    )
    return jnp.dot(activated, expert_out[0], preferred_element_type=jnp.float32).astype(
        jnp.bfloat16
    )


def shards(
    hidden_in,
    queries,
    latent_cache,
    lengths,
    w_uv,
    attn_weight,
    norm_gain,
    router,
    routes,
    live_counts,
    expert_in,
    expert_out,
):
    count_of_tokens, width = hidden_in.shape
    sections = lax.axis_size("sec")
    expert_groups = lax.axis_size(GRP)
    slices = lax.axis_size("tp")
    latent_width = w_uv.shape[2]
    query_block = queries[:, :, 0, :]
    scores = (
        jnp.einsum("bhr,bpr->bhp", query_block, latent_cache, preferred_element_type=jnp.float32)
        * score_scale
    )
    positions = jnp.arange(latent_cache.shape[1])
    visible = positions[None, None, :] < lengths[:, None, None]
    scores = jnp.where(visible, scores, -1e30)
    highest = jnp.max(scores, axis=2, keepdims=True)
    raised = jnp.exp(scores - highest)
    softmax_weights = (raised / jnp.sum(raised, axis=2, keepdims=True)).astype(jnp.bfloat16)
    latent_out = jnp.einsum(
        "bhp,bpc->bhc",
        softmax_weights,
        latent_cache[:, :, :latent_width],
        preferred_element_type=jnp.float32,
    ).astype(jnp.bfloat16)
    head_out = jnp.einsum(
        "bhc,hcv->bhv", latent_out, w_uv[:, 0], preferred_element_type=jnp.float32
    ).astype(jnp.bfloat16)
    head_rows = head_out.reshape(head_out.shape[0], -1)
    out_block = attn_weight[:, 0].reshape(-1, attn_weight.shape[3])
    partial_value = jnp.dot(
        gathered_by_axis(head_rows, GRP, 0), out_block, preferred_element_type=jnp.float32
    )
    partial_value = partial_value.reshape(
        expert_groups, slices, count_of_tokens, partial_value.shape[1]
    )
    summed = sent_and_summed(partial_value.astype(jnp.bfloat16), "tp", 1)
    column_part = summed[:, 0].astype(jnp.bfloat16)
    attention = lax.all_to_all(column_part, GRP, split_axis=0, concat_axis=2, tiled=True)[0]
    residual = hidden_in.astype(jnp.float32) + attention.astype(jnp.float32)
    normalized_input = (
        residual
        * lax.rsqrt(jnp.mean(residual * residual, axis=1, keepdims=True) + 1e-06)
        * norm_gain
    ).astype(jnp.bfloat16)
    experts = router.shape[1]
    per_token = routes.shape[1]
    capacity = max(2, 2 * count_of_tokens * per_token // experts)
    affinity = jax.nn.sigmoid(jnp.dot(normalized_input, router, preferred_element_type=jnp.float32))
    picked = routes[:, :, None] == jnp.arange(experts)[None, None, :]
    chosen = jnp.sum(jnp.where(picked, affinity[:, None, :], 0.0), axis=2)
    living = jnp.arange(count_of_tokens) < live_counts[0]
    gate_weights = (
        route_scale
        * chosen
        / jnp.sum(chosen, axis=1, keepdims=True)
        * living[:, None].astype(jnp.float32)
    )
    routed = jnp.any(picked, axis=1) & living[:, None]
    routed_count = routed.astype(jnp.int32)
    slot_index = jnp.cumsum(routed_count, axis=0) - routed_count
    placed_tokens = routed[:, :, None] & (
        slot_index[:, :, None] == jnp.arange(capacity)[None, None, :]
    )
    expert_gate = jnp.sum(jnp.where(picked, gate_weights[:, :, None], 0.0), axis=1)
    outgoing = jnp.einsum(
        "poy,pj->oyj",
        placed_tokens.astype(jnp.bfloat16),
        normalized_input,
        preferred_element_type=jnp.float32,
    ).astype(jnp.bfloat16)
    combine_rows = (placed_tokens.astype(jnp.float32) * expert_gate[:, :, None]).reshape(
        count_of_tokens, experts * capacity
    )
    once_rows = outgoing.reshape(sections, expert_groups, capacity, width)
    arrived = exchange_both(once_rows, SEC_GRP, ("sec", GRP), (0, 1), (0, 1))
    local_rows = arrived.reshape(-1, width)
    every_out = expert_slice(
        lax.all_gather(local_rows, "tp", axis=0, tiled=True), expert_in, expert_out
    )
    own_sums = lax.psum_scatter(
        every_out.astype(jnp.float32).astype(jnp.bfloat16), "tp", scatter_dimension=0, tiled=True
    ).astype(jnp.float32)
    own_sums = own_sums.reshape(sections, expert_groups, capacity, width)
    back_rows = exchange_both(
        own_sums.astype(jnp.bfloat16), GRP_SEC, (GRP, "sec"), (1, 0), (1, 0)
    ).astype(own_sums.dtype)
    expert_sums = back_rows.reshape(experts * capacity, width)
    expert_mix = jnp.dot(combine_rows, expert_sums, precision=lax.Precision.HIGHEST)
    return (residual + expert_mix).astype(jnp.bfloat16)


def solution(mesh):
    torus = Mesh(
        mesh.devices.reshape(mesh.shape["sec"], 8, 2, mesh.shape["tp"]),
        ("sec", "grp_0", "grp_1", "tp"),
    )
    in_specs = (
        P(SEC_GRP_TP, None),
        P(SEC_GRP, None, "tp", None),
        P(SEC_GRP, None, None),
        P(SEC_GRP),
        P(None, "tp", None, None),
        P(None, "tp", None, GRP),
        P(),
        P(),
        P(SEC_GRP_TP, None),
        P(SEC_GRP_TP),
        P(SEC_GRP, None, None, "tp"),
        P(SEC_GRP, "tp", None),
    )
    out_specs = P(SEC_GRP_TP, None)
    return jax.shard_map(
        shards, mesh=torus, in_specs=in_specs, out_specs=out_specs, check_vma=False
    )
```

profile of v0, /device:TPU:8, one launch (start us, length us, event | category | flops | bytes accessed | tf_op | source)
XLA Modules:
  0.0 292.9 jit_solution(1517495895846176154)
XLA Ops:
  7.4 2.9 fusion.29
  10.5 2.5 fusion.19
  13.7 7.5 %all_gather.9 = bf16[64,2048]{1,0:T(8,128)(2,1)} all-gather(bf16[32,2048]{1,0:T(8,128)(2,1)S(1)} %bitcast.86), channel_id=1, replica_groups=mesh['sec'=2,'grp_0'=8,'grp_1'=2,'tp'=8] {'grp_1'}, dimensions={0}, use_global_device_ids=true | all-gather | bytes 393216 | tf_op jit(solution)/shard_map/all_gather | solution.py:18
  21.9 3.9 %copy.34 = bf16[16,1,128,448]{2,0,3,1:T(8,128)(2,1)} copy(bf16[16,1,128,448]{2,3,1,0:T(8,128)(2,1)} %param.17) | data formatting | bytes 3670016 | tf_op args[5]
  25.9 3.9 %reshape.224 = bf16[2048,448,1,1]{0,1,2,3:T(8,128)(2,1)} reshape(bf16[16,1,128,448]{2,0,3,1:T(8,128)(2,1)} %copy.34) | data formatting | bytes 3670016 | tf_op jit(solution)/shard_map/reshape;squeeze | solution.py:105
  29.7 35.4 %all-gather.3.cloned.1.call-done = bf16[512,2048]{1,0:T(8,128)(2,1)} async-done(((bf16[64,2048]{1,0:T(8,128)(2,1)}), bf16[512,2048]{1,0:T(8,128)(2,1)}) %all-gather.3.cloned.1.call-update) | async-done | bytes 2097168 | tf_op jit(solution)/shard_map/all_gather | solution.py:18
  65.2 4.1 %dot_general.32 = bf16[16,8,4,2048]{3,2,1,0:T(4,128)(2,1)} reshape(bf16[512,2048]{1,0:T(8,128)(2,1)} %all-gather.3.cloned.1.call-done) | data formatting | bytes 4194304 | tf_op jit(solution)/shard_map/dot_general | solution.py:106
  69.3 3.6 %fusion.22 = bf16[8,16,1,4,448]{4,0,3,1,2:T(8,128)(2,1)S(1)} fusion(bf16[2048,448,1,1]{0,1,2,3:T(8,128)(2,1)} %reshape.224, bf16[16,8,4,2048]{3,2,1,0:T(4,128)(2,1)} %dot_general.32), kind=kOutput, calls=%fused_computation.19 | convolution fusion | flops 939753472 | bytes 4390912 | tf_op jit(solution)/shard_map/dot_general | solution.py:106
  74.0 4.3 %all-to-all-start = ((bf16[8,16,1,4,448]{4,3,1,2,0:T(4,128)(2,1)}), bf16[8,16,1,4,448]{4,3,1,2,0:T(4,128)(2,1)S(1)}, u32[]{:S(2)}, u32[]{:S(2)}) async-start(bf16[8,16,1,4,448]{4,3,1,2,0:T(4,128)(2,1)} %copy.36), calls=%async_computation | async-start | bytes 1048576 | tf_op jit(solution)/shard_map/all_to_all | solution.py:30
  78.5 10.1 %all-to-all-done = bf16[8,16,1,4,448]{4,3,1,2,0:T(4,128)(2,1)S(1)} async-done(((bf16[8,16,1,4,448]{4,3,1,2,0:T(4,128)(2,1)}), bf16[8,16,1,4,448]{4,3,1,2,0:T(4,128)(2,1)S(1)}, u32[]{:S(2)}, u32[]{:S(2)}) %all-to-all-start) | async-done | bytes 458784 | tf_op jit(solution)/shard_map/all_to_all | solution.py:30
  89.4 5.9 %all-to-all-start.1 = ((bf16[16,4,448]{2,1,0:T(4,128)(2,1)}), bf16[16,4,448]{2,1,0:T(4,128)(2,1)S(1)}, u32[]{:S(2)}, u32[]{:S(2)}) async-start(bf16[16,4,448]{2,1,0:T(4,128)(2,1)} %reduce_sum.58), calls=%async_computation.1 | async-start | bytes 131072 | tf_op jit(solution)/shard_map/all_to_all | solution.py:114
  95.6 10.3 %all-to-all-done.1 = bf16[16,4,448]{2,1,0:T(4,128)(2,1)S(1)} async-done(((bf16[16,4,448]{2,1,0:T(4,128)(2,1)}), bf16[16,4,448]{2,1,0:T(4,128)(2,1)S(1)}, u32[]{:S(2)}, u32[]{:S(2)}) %all-to-all-start.1) | async-done | bytes 57376 | tf_op jit(solution)/shard_map/all_to_all | solution.py:114
  106.4 1.2 fusion.38
  109.5 27.3 %all_to_all.24 = bf16[32,1,1,2,7168]{4,3,2,1,0:T(2,128)(2,1)S(1)} all-to-all(bf16[32,1,1,2,7168]{4,3,2,1,0:T(2,128)(2,1)S(1)} %copy.43), channel_id=1, replica_groups=mesh['sec'=2,'grp_0'=8,'grp_1'=2,'tp'=8] {'sec','grp_0','grp_1'}, dimensions={0} | all-to-all | bytes 1835008 | tf_op jit(solution)/shard_map/all_to_all | solution.py:46
  136.9 1.3 reshape_reshape.7
  138.4 43.3 %all-gather.5.cloned.1.call-done = bf16[512,7168]{1,0:T(8,128)(2,1)} async-done(((bf16[64,7168]{1,0:T(8,128)(2,1)}), bf16[512,7168]{1,0:T(8,128)(2,1)}) %all-gather.5.cloned.1.call-update) | async-done | bytes 7340048 | tf_op jit(solution)/shard_map/all_gather | solution.py:154
  181.7 6.3 %fusion.3 = f32[512,256]{1,0:T(8,128)S(1)} fusion(bf16[512,7168]{1,0:T(8,128)(2,1)} %all-gather.5.cloned.1.call-done, bf16[896,8,2,128]{3,2,1,0:T(2,128)(2,1)} %bitcast.88), kind=kOutput, calls=%fused_computation.6 | convolution fusion | flops 1879048192 | bytes 11534336 | tf_op jit(solution)/shard_map/dot_general | solution.py:54
  188.0 5.1 %convolution_convert_fusion = bf16[512,7168]{1,0:T(8,128)(2,1)} fusion(bf16[1,128,7168]{2,1,0:T(8,128)(2,1)S(1)} %copy-done.1, f32[512,256]{1,0:T(8,128)S(1)} %fusion.3), kind=kOutput, calls=%fused_computation.1 | convolution fusion | flops 943587328 | bytes 9699328 | tf_op jit(solution)/shard_map/dot_general | solution.py:60
  193.1 50.3 %reduce-scatter.2.cloned.1.call-done = bf16[64,7168]{1,0:T(8,128)(2,1)} async-done(((bf16[512,7168]{1,0:T(8,128)(2,1)}), bf16[64,7168]{1,0:T(8,128)(2,1)}) %reduce-scatter.2.cloned.1.call-update) | async-done | bytes 917520 | tf_op jit(solution)/shard_map/reduce_scatter | solution.py:156
  243.5 2.3 convert_element_type.99
  246.4 34.7 %all_to_all.25 = bf16[32,1,1,2,7168]{4,3,2,1,0:T(2,128)(2,1)S(1)} all-to-all(bf16[32,1,1,2,7168]{4,3,2,1,0:T(2,128)(2,1)S(1)} %bitcast.83), channel_id=1, replica_groups=mesh['sec'=2,'grp_0'=8,'grp_1'=2,'tp'=8] {'grp_0','grp_1','sec'}, dimensions={0} | all-to-all | bytes 1835008 | tf_op jit(solution)/shard_map/all_to_all | solution.py:46
  281.1 1.6 copy.67
  282.7 2.5 reshape.221
  285.2 1.2 fusion.2
  (43 shorter events, 7.3 us)
Async XLA Ops:
  6.5 6.6 %copy-start = (bf16[16,1,512,128]{3,2,1,0:T(8,128)(2,1)S(1)}, bf16[16,1,512,128]{3,2,1,0:T(8,128)(2,1)}, u32[]{:S(2)}) copy-start(bf16[16,1,512,128]{3,2,1,0:T(8,128)(2,1)} %param.16) | copy-start | bytes 6291460
  6.5 58.6 %all-gather.3.cloned.1.call-start = ((), (), s32[]{:S(2)}) async-start(), calls=%async_computation.5 | async-start | bytes 2359296 | tf_op jit(solution)/shard_map/all_gather | solution.py:18
  72.9 5.4 %copy-start.4 = (s32[4,8]{1,0:T(4,128)S(1)}, s32[4,8]{1,0:T(4,128)}, u32[]{:S(2)}) copy-start(s32[4,8]{1,0:T(4,128)} %param.20) | copy-start | bytes 388
  72.9 33.2 %copy-start.2 = (bf16[4,7168]{1,0:T(4,128)(2,1)S(1)}, bf16[4,7168]{1,0:T(4,128)(2,1)}, u32[]{:S(2)}) copy-start(bf16[4,7168]{1,0:T(4,128)(2,1)} %param.12) | copy-start | bytes 172036
  72.9 33.4 %copy-start.3 = (f32[7168]{0:T(1024)S(1)}, f32[7168]{0:T(1024)}, u32[]{:S(2)}) copy-start(f32[7168]{0:T(1024)} %param.18) | copy-start | bytes 86020
  74.0 14.6 %all-to-all-start = ((bf16[8,16,1,4,448]{4,3,1,2,0:T(4,128)(2,1)}), bf16[8,16,1,4,448]{4,3,1,2,0:T(4,128)(2,1)S(1)}, u32[]{:S(2)}, u32[]{:S(2)}) async-start(bf16[8,16,1,4,448]{4,3,1,2,0:T(4,128)(2,1)} %copy.36), calls=%async_computation | async-start | bytes 1048576 | tf_op jit(solution)/shard_map/all_to_all | solution.py:30
  89.4 16.5 %all-to-all-start.1 = ((bf16[16,4,448]{2,1,0:T(4,128)(2,1)}), bf16[16,4,448]{2,1,0:T(4,128)(2,1)S(1)}, u32[]{:S(2)}, u32[]{:S(2)}) async-start(bf16[16,4,448]{2,1,0:T(4,128)(2,1)} %reduce_sum.58), calls=%async_computation.1 | async-start | bytes 131072 | tf_op jit(solution)/shard_map/all_to_all | solution.py:114
  95.4 86.3 %all-gather.5.cloned.1.call-start = ((), (), s32[]{:S(2)}) async-start(), calls=%async_computation.6 | async-start | bytes 8257536 | tf_op jit(solution)/shard_map/all_gather | solution.py:154
  138.1 105.3 %reduce-scatter.2.cloned.1.call-start = ((), (), s32[]{:S(2)}) async-start(), calls=%async_computation.7 | async-start | bytes 8257536 | tf_op jit(solution)/shard_map/reduce_scatter | solution.py:156
  181.7 6.3 %copy-start.1 = (bf16[1,128,7168]{2,1,0:T(8,128)(2,1)S(1)}, bf16[1,128,7168]{2,1,0:T(8,128)(2,1)}, u32[]{:S(2)}) copy-start(bf16[1,128,7168]{2,1,0:T(8,128)(2,1)} %param.23) | copy-start | bytes 5505028
Sparse Core Ops, SparseCore 0:
  21.4 43.7 all-gather.2
  138.3 43.3 all-gather.4
  193.2 50.1 reduce-scatter.1
where the time goes:
time: 294 us; the launch traced here: 293 us
  waiting for transfers between devices  150 us (51%)
  blocking collectives  69.6 us (24%)
  matrix products  23.8 us (8%)
  local copies, waits for them, and re-layouts  22.7 us (8%)
  between operations  14 us (5%)
  starting transfers between devices  10.5 us (4%)
    all_to_all x2, blocking collectives, exchange_both(): tiles = lax.all_to_all(tiles, axis, split_axis=0, concat_axis=0, tiled=True)  62 us
    reduce_scatter x1, waiting for transfers between devices, shards(): lax.psum_scatter(every_out.astype(jnp.float32).astype(jnp.bfloat16), 'tp'...  50.3 us
    all_gather x1, waiting for transfers between devices, shards(): lax.all_gather(local_rows, 'tp', axis=0, tiled=True)  43.3 us
    all_gather x1, waiting for transfers between devices, gathered_by_axis(): out = lax.all_gather(out, axes[number], axis=dim, tiled=True)  35.4 us
    all_to_all x1, waiting for transfers between devices, shards(): lax.all_to_all(column_part, GRP, split_axis=0, concat_axis=2, tiled=True)[0]  10.3 us
    all_to_all x1, waiting for transfers between devices, sent_and_summed(): lax.all_to_all(tiles, axis, split_axis=0, concat_axis=0, tiled=True)  10.1 us
    all_gather x1, blocking collectives, gathered_by_axis(): out = lax.all_gather(out, axes[number], axis=dim, tiled=True)  7.51 us
    dot_general x1, matrix products, expert_slice(): jnp.dot(rows_in, expert_in[0].reshape(width, 2 * slice_width), preferred_...  6.32 us
  transfers between devices with their start and end apart: 5, of which 5 were waited for; matrix products, arithmetic and copies ran while one was open for 3% of the time, Pallas kernels for 0%

commit v1 on v0

--- a/solution.py
+++ b/solution.py
@@ -111,7 +111,10 @@
     )
     summed = sent_and_summed(partial_value.astype(jnp.bfloat16), "tp", 1)
     column_part = summed[:, 0].astype(jnp.bfloat16)
-    attention = lax.all_to_all(column_part, GRP, split_axis=0, concat_axis=2, tiled=True)[0]
+    attention = jnp.concatenate(
+        lax.all_to_all(jnp.stack(jnp.split(column_part, lax.axis_size(GRP), axis=0)), GRP, 0, 0),
+        axis=2,
+    )[0]
     residual = hidden_in.astype(jnp.float32) + attention.astype(jnp.float32)
     normalized_input = (
         residual

time: 294 us -> 302 us (1.027)
  local copies, waits for them, and re-layouts: 22.7 us -> 32.2 us
    unnamed x11 -> x26, local copies, waits for them, and re-layouts: 3.95 us -> 12.9 us
where the time goes in v1:
time: 302 us
  waiting for transfers between devices  150 us (50%)
  blocking collectives  69.5 us (23%)
  local copies, waits for them, and re-layouts  32.2 us (11%)
  matrix products  23.8 us (8%)
  between operations  14 us (5%)
  starting transfers between devices  10.5 us (3%)
    all_to_all x2, blocking collectives, exchange_both(): tiles = lax.all_to_all(tiles, axis, split_axis=0, concat_axis=0, tiled=True)  62 us
    reduce_scatter x1, waiting for transfers between devices, shards(): lax.psum_scatter(every_out.astype(jnp.float32).astype(jnp.bfloat16), 'tp'...  50.3 us
    all_gather x1, waiting for transfers between devices, shards(): lax.all_gather(local_rows, 'tp', axis=0, tiled=True)  43.3 us
    all_gather x1, waiting for transfers between devices, gathered_by_axis(): out = lax.all_gather(out, axes[number], axis=dim, tiled=True)  35.4 us
    unnamed x26, local copies, waits for them, and re-layouts  12.9 us
    all_to_all x1, waiting for transfers between devices, shards(): lax.all_to_all(jnp.stack(jnp.split(column_part, lax.axis_size(GRP), axis=...  10.3 us
    all_to_all x1, waiting for transfers between devices, sent_and_summed(): lax.all_to_all(tiles, axis, split_axis=0, concat_axis=0, tiled=True)  10.1 us
    all_gather x1, blocking collectives, gathered_by_axis(): out = lax.all_gather(out, axes[number], axis=dim, tiled=True)  7.51 us
  transfers between devices with their start and end apart: 5, of which 5 were waited for; matrix products, arithmetic and copies ran while one was open for 3% of the time, Pallas kernels for 0%

profile of v1, /device:TPU:8, one launch (start us, length us, event | category | flops | bytes accessed | tf_op | source)
XLA Modules:
  0.0 301.7 jit_solution(16221769283066514143)
XLA Ops:
  7.4 2.9 fusion.29
  10.5 2.5 fusion.19
  13.7 7.5 %all_gather.9 = bf16[64,2048]{1,0:T(8,128)(2,1)} all-gather(bf16[32,2048]{1,0:T(8,128)(2,1)S(1)} %bitcast.147), channel_id=1, replica_groups=mesh['sec'=2,'grp_0'=8,'grp_1'=2,'tp'=8] {'grp_1'}, dimensions={0}, use_global_device_ids=true | all-gather | bytes 393216 | tf_op jit(solution)/shard_map/all_gather | solution.py:18
  21.9 3.9 %copy.49 = bf16[16,1,128,448]{2,0,3,1:T(8,128)(2,1)} copy(bf16[16,1,128,448]{2,3,1,0:T(8,128)(2,1)} %param.17) | data formatting | bytes 3670016 | tf_op args[5]
  25.9 3.9 %reshape.221 = bf16[2048,448,1,1]{0,1,2,3:T(8,128)(2,1)} reshape(bf16[16,1,128,448]{2,0,3,1:T(8,128)(2,1)} %copy.49) | data formatting | bytes 3670016 | tf_op jit(solution)/shard_map/reshape;squeeze | solution.py:105
  29.7 35.4 %all-gather.3.cloned.1.call-done = bf16[512,2048]{1,0:T(8,128)(2,1)} async-done(((bf16[64,2048]{1,0:T(8,128)(2,1)}), bf16[512,2048]{1,0:T(8,128)(2,1)}) %all-gather.3.cloned.1.call-update) | async-done | bytes 2097168 | tf_op jit(solution)/shard_map/all_gather | solution.py:18
  65.2 4.1 %dot_general.32 = bf16[16,8,4,2048]{3,2,1,0:T(4,128)(2,1)} reshape(bf16[512,2048]{1,0:T(8,128)(2,1)} %all-gather.3.cloned.1.call-done) | data formatting | bytes 4194304 | tf_op jit(solution)/shard_map/dot_general | solution.py:106
  69.3 3.6 %fusion.22 = bf16[8,16,1,4,448]{4,0,3,1,2:T(8,128)(2,1)S(1)} fusion(bf16[2048,448,1,1]{0,1,2,3:T(8,128)(2,1)} %reshape.221, bf16[16,8,4,2048]{3,2,1,0:T(4,128)(2,1)} %dot_general.32), kind=kOutput, calls=%fused_computation.19 | convolution fusion | flops 939753472 | bytes 4390912 | tf_op jit(solution)/shard_map/dot_general | solution.py:106
  74.0 4.3 %all-to-all-start = ((bf16[8,16,1,4,448]{4,3,1,2,0:T(4,128)(2,1)}), bf16[8,16,1,4,448]{4,3,1,2,0:T(4,128)(2,1)S(1)}, u32[]{:S(2)}, u32[]{:S(2)}) async-start(bf16[8,16,1,4,448]{4,3,1,2,0:T(4,128)(2,1)} %copy.51), calls=%async_computation | async-start | bytes 1048576 | tf_op jit(solution)/shard_map/all_to_all | solution.py:30
  78.5 10.1 %all-to-all-done = bf16[8,16,1,4,448]{4,3,1,2,0:T(4,128)(2,1)S(1)} async-done(((bf16[8,16,1,4,448]{4,3,1,2,0:T(4,128)(2,1)}), bf16[8,16,1,4,448]{4,3,1,2,0:T(4,128)(2,1)S(1)}, u32[]{:S(2)}, u32[]{:S(2)}) %all-to-all-start) | async-done | bytes 458784 | tf_op jit(solution)/shard_map/all_to_all | solution.py:30
  98.3 5.9 %all-to-all-start.1 = ((bf16[16,1,4,448]{3,2,1,0:T(4,128)(2,1)}), bf16[16,1,4,448]{3,2,1,0:T(4,128)(2,1)S(1)}, u32[]{:S(2)}, u32[]{:S(2)}) async-start(bf16[16,1,4,448]{3,2,1,0:T(4,128)(2,1)} %constant_dynamic-update-slice_fusion), calls=%async_computation.1 | async-start | bytes 131072 | tf_op jit(solution)/shard_map/all_to_all | solution.py:115
  104.5 10.3 %all-to-all-done.1 = bf16[16,1,4,448]{3,2,1,0:T(4,128)(2,1)S(1)} async-done(((bf16[16,1,4,448]{3,2,1,0:T(4,128)(2,1)}), bf16[16,1,4,448]{3,2,1,0:T(4,128)(2,1)S(1)}, u32[]{:S(2)}, u32[]{:S(2)}) %all-to-all-start.1) | async-done | bytes 57376 | tf_op jit(solution)/shard_map/all_to_all | solution.py:115
  115.3 1.2 fusion.38
  118.4 27.3 %all_to_all.20 = bf16[32,1,1,2,7168]{4,3,2,1,0:T(2,128)(2,1)S(1)} all-to-all(bf16[32,1,1,2,7168]{4,3,2,1,0:T(2,128)(2,1)S(1)} %copy.57), channel_id=1, replica_groups=mesh['sec'=2,'grp_0'=8,'grp_1'=2,'tp'=8] {'sec','grp_0','grp_1'}, dimensions={0} | all-to-all | bytes 1835008 | tf_op jit(solution)/shard_map/all_to_all | solution.py:46
  145.7 1.3 reshape_reshape.7
  147.3 43.3 %all-gather.5.cloned.1.call-done = bf16[512,7168]{1,0:T(8,128)(2,1)} async-done(((bf16[64,7168]{1,0:T(8,128)(2,1)}), bf16[512,7168]{1,0:T(8,128)(2,1)}) %all-gather.5.cloned.1.call-update) | async-done | bytes 7340048 | tf_op jit(solution)/shard_map/all_gather | solution.py:157
  190.6 6.3 %fusion.3 = f32[512,256]{1,0:T(8,128)S(1)} fusion(bf16[512,7168]{1,0:T(8,128)(2,1)} %all-gather.5.cloned.1.call-done, bf16[896,8,2,128]{3,2,1,0:T(2,128)(2,1)} %bitcast.149), kind=kOutput, calls=%fused_computation.6 | convolution fusion | flops 1879048192 | bytes 11534336 | tf_op jit(solution)/shard_map/dot_general | solution.py:54
  196.9 5.1 %convolution_convert_fusion = bf16[512,7168]{1,0:T(8,128)(2,1)} fusion(bf16[1,128,7168]{2,1,0:T(8,128)(2,1)S(1)} %copy-done.1, f32[512,256]{1,0:T(8,128)S(1)} %fusion.3), kind=kOutput, calls=%fused_computation.1 | convolution fusion | flops 943587328 | bytes 9699328 | tf_op jit(solution)/shard_map/dot_general | solution.py:60
  202.0 50.3 %reduce-scatter.2.cloned.1.call-done = bf16[64,7168]{1,0:T(8,128)(2,1)} async-done(((bf16[512,7168]{1,0:T(8,128)(2,1)}), bf16[64,7168]{1,0:T(8,128)(2,1)}) %reduce-scatter.2.cloned.1.call-update) | async-done | bytes 917520 | tf_op jit(solution)/shard_map/reduce_scatter | solution.py:159
  252.3 2.3 convert_element_type.95
  255.3 34.7 %all_to_all.21 = bf16[32,1,1,2,7168]{4,3,2,1,0:T(2,128)(2,1)S(1)} all-to-all(bf16[32,1,1,2,7168]{4,3,2,1,0:T(2,128)(2,1)S(1)} %bitcast.144), channel_id=1, replica_groups=mesh['sec'=2,'grp_0'=8,'grp_1'=2,'tp'=8] {'grp_0','grp_1','sec'}, dimensions={0} | all-to-all | bytes 1835008 | tf_op jit(solution)/shard_map/all_to_all | solution.py:46
  290.0 1.6 copy.80
  291.6 2.5 reshape.219
  294.0 1.2 fusion.2
  (59 shorter events, 16.2 us)
Async XLA Ops:
  6.5 6.6 %copy-start = (bf16[16,1,512,128]{3,2,1,0:T(8,128)(2,1)S(1)}, bf16[16,1,512,128]{3,2,1,0:T(8,128)(2,1)}, u32[]{:S(2)}) copy-start(bf16[16,1,512,128]{3,2,1,0:T(8,128)(2,1)} %param.16) | copy-start | bytes 6291460
  6.5 58.6 %all-gather.3.cloned.1.call-start = ((), (), s32[]{:S(2)}) async-start(), calls=%async_computation.5 | async-start | bytes 2359296 | tf_op jit(solution)/shard_map/all_gather | solution.py:18
  72.9 5.4 %copy-start.4 = (s32[4,8]{1,0:T(4,128)S(1)}, s32[4,8]{1,0:T(4,128)}, u32[]{:S(2)}) copy-start(s32[4,8]{1,0:T(4,128)} %param.20) | copy-start | bytes 388
  72.9 42.1 %copy-start.2 = (bf16[4,7168]{1,0:T(4,128)(2,1)S(1)}, bf16[4,7168]{1,0:T(4,128)(2,1)}, u32[]{:S(2)}) copy-start(bf16[4,7168]{1,0:T(4,128)(2,1)} %param.12) | copy-start | bytes 172036
  72.9 42.3 %copy-start.3 = (f32[7168]{0:T(1024)S(1)}, f32[7168]{0:T(1024)}, u32[]{:S(2)}) copy-start(f32[7168]{0:T(1024)} %param.18) | copy-start | bytes 86020
  74.0 14.6 %all-to-all-start = ((bf16[8,16,1,4,448]{4,3,1,2,0:T(4,128)(2,1)}), bf16[8,16,1,4,448]{4,3,1,2,0:T(4,128)(2,1)S(1)}, u32[]{:S(2)}, u32[]{:S(2)}) async-start(bf16[8,16,1,4,448]{4,3,1,2,0:T(4,128)(2,1)} %copy.51), calls=%async_computation | async-start | bytes 1048576 | tf_op jit(solution)/shard_map/all_to_all | solution.py:30
  98.3 16.5 %all-to-all-start.1 = ((bf16[16,1,4,448]{3,2,1,0:T(4,128)(2,1)}), bf16[16,1,4,448]{3,2,1,0:T(4,128)(2,1)S(1)}, u32[]{:S(2)}, u32[]{:S(2)}) async-start(bf16[16,1,4,448]{3,2,1,0:T(4,128)(2,1)} %constant_dynamic-update-slice_fusion), calls=%async_computation.1 | async-start | bytes 131072 | tf_op jit(solution)/shard_map/all_to_all | solution.py:115
  104.3 86.3 %all-gather.5.cloned.1.call-start = ((), (), s32[]{:S(2)}) async-start(), calls=%async_computation.6 | async-start | bytes 8257536 | tf_op jit(solution)/shard_map/all_gather | solution.py:157
  147.0 105.3 %reduce-scatter.2.cloned.1.call-start = ((), (), s32[]{:S(2)}) async-start(), calls=%async_computation.7 | async-start | bytes 8257536 | tf_op jit(solution)/shard_map/reduce_scatter | solution.py:159
  190.6 6.3 %copy-start.1 = (bf16[1,128,7168]{2,1,0:T(8,128)(2,1)S(1)}, bf16[1,128,7168]{2,1,0:T(8,128)(2,1)}, u32[]{:S(2)}) copy-start(bf16[1,128,7168]{2,1,0:T(8,128)(2,1)} %param.23) | copy-start | bytes 5505028
Sparse Core Ops, SparseCore 0:
  21.4 43.7 all-gather.2
  147.2 43.3 all-gather.4
  202.1 50.1 reduce-scatter.1
